TPU v7x, 768 devices: a whole 4x8x12 slice. The times are simulated.
768 devices in a mesh: space: 12 (over z), member: 64 (over x, y, core).
Axes of the slice: x: 4, y: 8, z: 12, core: 2. Of those that a mesh axis runs over, the one named last changes fastest.
Arguments:
- prior_ensemble: float32 [256, 256, 1536], P('member', None, 'space'), may hold values from -12 to 12, as said below
- wind: float32 [256, 1536], P(None, 'space'), may hold values from -1 to 1
- obs_value: float32 [768, 512], P(('space', 'member')), may hold values from -6 to 6
- obs_weight: float32 [768, 512], P(('space', 'member')), may hold values from 0.25 to 4
- observed_cell_value: int32 [768, 512], P(('space', 'member')), may hold values from 0 to 511
- obs_count: int32 [768], P(('space', 'member')), may hold values from 64 to 512, as said below
Outputs:
- analysis: float32 [256, 256, 1536], P('member', None, 'space')
Inputs may be any that keep to these rules, and one draw needn't show every extreme that they name: `prior_ensemble`: member states are rough from cell to cell, member scales differ. `obs_count`: some patch has all 512 slots live and some has 64 live.
All inputs are finite; a program needn't handle non-finite values.
Results may differ from a plain program's by a relative error of at most 0.0003.
Values sent between devices are 32-bit elements; how exact they have to be, the bound alone decides.
A program may use at most 32 MiB of HBM per device.

v0:
```python
import jax
import jax.numpy as jnp
from jax import lax
from jax.sharding import PartitionSpec as P

SUBSTEPS = 4
NS_ITERS = 6


def padded_2(block, sides, width):
    for axis, dim in sides:
        count = lax.axis_size(axis)
        forward = [(i, i + 1) for i in range(count - 1)]
        forward.append((count - 1, 0))
        backward = [(target, source) for source, target in forward]
        low = lax.ppermute(
            lax.slice_in_dim(block, block.shape[dim] - width, None, axis=dim), axis, forward
        )
        high = lax.ppermute(lax.slice_in_dim(block, 0, width, axis=dim), axis, backward)
        block = jnp.concatenate([low, block, high], axis=dim)
    return block


def tendency(center, east, west, wind_mid):
    pads = [(0, 0)] * (center.ndim - 2) + [(1, 1), (0, 0)]
    ypad = jnp.pad(center, pads)
    north = ypad[..., 2:, :]
    south = ypad[..., :-2, :]
    speed = wind_mid + 0.25 * jnp.tanh(center)
    return (
        center
        + 0.2 * (east - 2.0 * center + west)
        + 0.1 * (north - 2.0 * center + south)
        - 0.3 * speed * (east - west)
    )


def inverse_root(gram):
    order = gram.shape[0]
    ident = jnp.eye(order, dtype=jnp.float32)
    scale = jnp.sqrt(jnp.sum(gram * gram) + 1e-06)
    upper = gram / scale
    lower = ident
    for step in range(NS_ITERS):
        middle = 1.5 * ident - 0.5 * jnp.dot(lower, upper, precision=lax.Precision.HIGHEST)
        upper = jnp.dot(upper, middle, precision=lax.Precision.HIGHEST)
        lower = jnp.dot(middle, lower, precision=lax.Precision.HIGHEST)
    return lower / jnp.sqrt(scale)


def analyze(xb, cells, value, weight, count):
    order = xb.shape[0]
    slots = cells.shape[0]
    mean = jnp.sum(xb, axis=0) / order
    pert = xb - mean
    start_gram = (order - 1.0) * jnp.eye(order, dtype=jnp.float32)
    ypert = jnp.take(pert, cells, axis=1)
    ymean = jnp.take(mean, cells)
    live = (jnp.arange(slots, dtype=jnp.int32) < count).astype(jnp.float32)
    wts = weight * live
    gram = start_gram + jnp.dot(ypert * wts, ypert.T, precision=lax.Precision.HIGHEST)
    rhs = jnp.dot(ypert, wts * (value - ymean), precision=lax.Precision.HIGHEST)
    root = inverse_root(gram)
    wbar = jnp.dot(
        root, jnp.dot(root, rhs, precision=lax.Precision.HIGHEST), precision=lax.Precision.HIGHEST
    )
    trans = jnp.sqrt(order - 1.0) * root + wbar[:, None]
    return mean + jnp.dot(trans.T, pert, precision=lax.Precision.HIGHEST)


def local(prior_ensemble, wind, obs_value, obs_weight, observed_cell_value, obs_count):
    model_variable = prior_ensemble
    for step in range(SUBSTEPS):
        padded = padded_2(model_variable, (("space", 2),), 1)
        model_variable = tendency(padded[..., 1:-1], padded[..., 2:], padded[..., :-2], wind)
    mem_here, latitude_lines, column_entries = model_variable.shape
    groups = lax.axis_size("member")
    per_dev = obs_count.shape[0]
    cell_count = latitude_lines * column_entries // (groups * per_dev)
    blocks = model_variable.reshape(mem_here, groups, per_dev, cell_count)
    arrived = lax.all_to_all(blocks, "member", split_axis=1, concat_axis=0, tiled=True)
    output_results = [
        analyze(arrived[:, 0, 0], observed_cell_value[0], obs_value[0], obs_weight[0], obs_count[0])
    ]
    analysed_state = jnp.stack(output_results, axis=1)[:, None]
    returned = lax.all_to_all(analysed_state, "member", split_axis=0, concat_axis=1, tiled=True)
    return returned.reshape(mem_here, latitude_lines, column_entries)


def solution(mesh):
    in_specs = (
        P("member", None, "space"),
        P(None, "space"),
        P(("space", "member"), None),
        P(("space", "member"), None),
        P(("space", "member"), None),
        P(("space", "member")),
    )
    out_specs = P("member", None, "space")
    return jax.shard_map(local, mesh=mesh, in_specs=in_specs, out_specs=out_specs, check_vma=False)
```

profile of v0, /device:TPU:1, one launch (start us, length us, event | category | flops | bytes accessed | tf_op | source)
XLA Modules:
  0.0 158.1 jit_solution(10487588906502451167)
XLA Ops:
  0.0 1.5 fusion.27
  1.6 15.1 %collective-permute-start = (f32[4,256,1]{2,1,0:T(8,128)S(1)}, f32[4,256,1]{2,1,0:T(8,128)S(1)}, u32[]{:S(2)}, u32[]{:S(2)}) collective-permute-start(f32[4,256,1]{2,1,0:T(8,128)S(1)} %get-tuple-element.13), channel_id=1, source_target_pairs={{64,0},{128,64},{192,128},{256,192},{320,256},{384,320},{448,384},... | collective-permute-start | bytes 12296 | tf_op jit(solution)/shard_map/ppermute | solution.py:19
  16.7 1.9 %collective-permute-start.1 = (f32[4,256,1]{2,1,0:T(8,128)S(1)}, f32[4,256,1]{2,1,0:T(8,128)S(1)}, u32[]{:S(2)}, u32[]{:S(2)}) collective-permute-start(f32[4,256,1]{2,1,0:T(8,128)S(1)} %get-tuple-element.14), channel_id=1, source_target_pairs={{0,64},{64,128},{128,192},{192,256},{256,320},{320,384},{384,448},... | collective-permute-start | bytes 12296 | tf_op jit(solution)/shard_map/ppermute | solution.py:16
  18.6 8.7 %collective-permute-done = f32[4,256,1]{2,1,0:T(8,128)S(1)} collective-permute-done((f32[4,256,1]{2,1,0:T(8,128)S(1)}, f32[4,256,1]{2,1,0:T(8,128)S(1)}, u32[]{:S(2)}, u32[]{:S(2)}) %collective-permute-start) | collective-permute-done | bytes 4128 | tf_op jit(solution)/shard_map/ppermute | solution.py:19
  27.3 5.0 %collective-permute-done.1 = f32[4,256,1]{2,1,0:T(8,128)S(1)} collective-permute-done((f32[4,256,1]{2,1,0:T(8,128)S(1)}, f32[4,256,1]{2,1,0:T(8,128)S(1)}, u32[]{:S(2)}, u32[]{:S(2)}) %collective-permute-start.1) | collective-permute-done | bytes 4128 | tf_op jit(solution)/shard_map/ppermute | solution.py:16
  32.3 0.6 multiply_subtract_fusion.3
  33.1 1.9 %collective-permute-start.2 = (f32[4,256,1]{2,1,0:T(8,128)S(1)}, f32[4,256,1]{2,1,0:T(8,128)S(1)}, u32[]{:S(2)}, u32[]{:S(2)}) collective-permute-start(f32[4,256,1]{2,1,0:T(8,128)S(1)} %get-tuple-element.11), channel_id=1, source_target_pairs={{64,0},{128,64},{192,128},{256,192},{320,256},{384,320},{448,384},... | collective-permute-start | bytes 12296 | tf_op jit(solution)/shard_map/ppermute | solution.py:19
  35.0 3.4 %collective-permute-start.3 = (f32[4,256,1]{2,1,0:T(8,128)S(1)}, f32[4,256,1]{2,1,0:T(8,128)S(1)}, u32[]{:S(2)}, u32[]{:S(2)}) collective-permute-start(f32[4,256,1]{2,1,0:T(8,128)S(1)} %get-tuple-element.12), channel_id=1, source_target_pairs={{0,64},{64,128},{128,192},{192,256},{256,320},{320,384},{384,448},... | collective-permute-start | bytes 12296 | tf_op jit(solution)/shard_map/ppermute | solution.py:16
  38.4 8.3 %collective-permute-done.2 = f32[4,256,1]{2,1,0:T(8,128)S(1)} collective-permute-done((f32[4,256,1]{2,1,0:T(8,128)S(1)}, f32[4,256,1]{2,1,0:T(8,128)S(1)}, u32[]{:S(2)}, u32[]{:S(2)}) %collective-permute-start.2) | collective-permute-done | bytes 4128 | tf_op jit(solution)/shard_map/ppermute | solution.py:19
  46.7 3.1 %collective-permute-done.3 = f32[4,256,1]{2,1,0:T(8,128)S(1)} collective-permute-done((f32[4,256,1]{2,1,0:T(8,128)S(1)}, f32[4,256,1]{2,1,0:T(8,128)S(1)}, u32[]{:S(2)}, u32[]{:S(2)}) %collective-permute-start.3) | collective-permute-done | bytes 4128 | tf_op jit(solution)/shard_map/ppermute | solution.py:16
  49.8 0.6 multiply_subtract_fusion.2
  50.6 1.9 %collective-permute-start.4 = (f32[4,256,1]{2,1,0:T(8,128)S(1)}, f32[4,256,1]{2,1,0:T(8,128)S(1)}, u32[]{:S(2)}, u32[]{:S(2)}) collective-permute-start(f32[4,256,1]{2,1,0:T(8,128)S(1)} %get-tuple-element.9), channel_id=1, source_target_pairs={{64,0},{128,64},{192,128},{256,192},{320,256},{384,320},{448,384},... | collective-permute-start | bytes 12296 | tf_op jit(solution)/shard_map/ppermute | solution.py:19
  52.5 3.4 %collective-permute-start.5 = (f32[4,256,1]{2,1,0:T(8,128)S(1)}, f32[4,256,1]{2,1,0:T(8,128)S(1)}, u32[]{:S(2)}, u32[]{:S(2)}) collective-permute-start(f32[4,256,1]{2,1,0:T(8,128)S(1)} %get-tuple-element.10), channel_id=1, source_target_pairs={{0,64},{64,128},{128,192},{192,256},{256,320},{320,384},{384,448},... | collective-permute-start | bytes 12296 | tf_op jit(solution)/shard_map/ppermute | solution.py:16
  55.9 7.4 %collective-permute-done.4 = f32[4,256,1]{2,1,0:T(8,128)S(1)} collective-permute-done((f32[4,256,1]{2,1,0:T(8,128)S(1)}, f32[4,256,1]{2,1,0:T(8,128)S(1)}, u32[]{:S(2)}, u32[]{:S(2)}) %collective-permute-start.4) | collective-permute-done | bytes 4128 | tf_op jit(solution)/shard_map/ppermute | solution.py:19
  63.3 3.1 %collective-permute-done.5 = f32[4,256,1]{2,1,0:T(8,128)S(1)} collective-permute-done((f32[4,256,1]{2,1,0:T(8,128)S(1)}, f32[4,256,1]{2,1,0:T(8,128)S(1)}, u32[]{:S(2)}, u32[]{:S(2)}) %collective-permute-start.5) | collective-permute-done | bytes 4128 | tf_op jit(solution)/shard_map/ppermute | solution.py:16
  66.5 0.6 multiply_subtract_fusion.1
  67.2 1.9 %collective-permute-start.6 = (f32[4,256,1]{2,1,0:T(8,128)S(1)}, f32[4,256,1]{2,1,0:T(8,128)S(1)}, u32[]{:S(2)}, u32[]{:S(2)}) collective-permute-start(f32[4,256,1]{2,1,0:T(8,128)S(1)} %get-tuple-element.7), channel_id=1, source_target_pairs={{64,0},{128,64},{192,128},{256,192},{320,256},{384,320},{448,384},... | collective-permute-start | bytes 12296 | tf_op jit(solution)/shard_map/ppermute | solution.py:19
  69.2 3.4 %collective-permute-start.7 = (f32[4,256,1]{2,1,0:T(8,128)S(1)}, f32[4,256,1]{2,1,0:T(8,128)S(1)}, u32[]{:S(2)}, u32[]{:S(2)}) collective-permute-start(f32[4,256,1]{2,1,0:T(8,128)S(1)} %get-tuple-element.8), channel_id=1, source_target_pairs={{0,64},{64,128},{128,192},{192,256},{256,320},{320,384},{384,448},... | collective-permute-start | bytes 12296 | tf_op jit(solution)/shard_map/ppermute | solution.py:16
  72.5 6.6 %collective-permute-done.6 = f32[4,256,1]{2,1,0:T(8,128)S(1)} collective-permute-done((f32[4,256,1]{2,1,0:T(8,128)S(1)}, f32[4,256,1]{2,1,0:T(8,128)S(1)}, u32[]{:S(2)}, u32[]{:S(2)}) %collective-permute-start.6) | collective-permute-done | bytes 4128 | tf_op jit(solution)/shard_map/ppermute | solution.py:19
  79.1 3.1 %collective-permute-done.7 = f32[4,256,1]{2,1,0:T(8,128)S(1)} collective-permute-done((f32[4,256,1]{2,1,0:T(8,128)S(1)}, f32[4,256,1]{2,1,0:T(8,128)S(1)}, u32[]{:S(2)}, u32[]{:S(2)}) %collective-permute-start.7) | collective-permute-done | bytes 4128 | tf_op jit(solution)/shard_map/ppermute | solution.py:16
  82.2 0.6 multiply_subtract_fusion
  82.9 1.1 copy.16
  84.0 14.6 %all-to-all-start = ((f32[4,64,1,512]{3,0,2,1:T(4,128)}), f32[4,64,1,512]{3,0,2,1:T(4,128)S(1)}, u32[]{:S(2)}, u32[]{:S(2)}) async-start(f32[4,64,1,512]{3,0,2,1:T(4,128)} %copy.16), calls=%async_computation | async-start | bytes 1048576 | tf_op jit(solution)/shard_map/all_to_all | solution.py:81
  99.4 16.6 %all-to-all-done = f32[4,64,1,512]{3,0,2,1:T(4,128)S(1)} async-done(((f32[4,64,1,512]{3,0,2,1:T(4,128)}), f32[4,64,1,512]{3,0,2,1:T(4,128)S(1)}, u32[]{:S(2)}, u32[]{:S(2)}) %all-to-all-start) | async-done | bytes 524320 | tf_op jit(solution)/shard_map/all_to_all | solution.py:81
  116.5 3.5 %gather_fusion.1 = f32[512]{0:T(512)S(1)} fusion(f32[512]{0:T(512)S(1)} %broadcast_multiply_fusion, s32[1024]{0:T(1024)S(1)} %pad_clamp_fusion), kind=kCustom, calls=%fused_computation.1 | custom fusion | bytes 6144 | tf_op jit(solution)/shard_map/jit(_take)/gather | solution.py:58
  120.0 1.6 gather_fusion
  121.6 0.7 copy-done.4
  122.3 1.9 %multiply_reduce_fusion = (f32[]{:T(128)}, f32[256,256]{1,0:T(8,128)S(1)}) fusion(f32[512,256]{1,0:T(8,128)S(1)} %gather_fusion, pred[512]{0:T(512)(128)(4,1)S(1)} %get-tuple-element.6, f32[512]{0:T(512)S(1)} %bitcast.76), kind=kOutput, calls=%fused_computation.40 | convolution fusion | flops 403374080 | bytes 788996 | tf_op jit(solution)/shard_map/dot_general | solution.py:61
  132.4 0.8 fusion
  133.2 0.5 copy.18
  133.7 23.4 %all_to_all.30 = f32[256,1,1,512]{3,2,1,0:T(1,128)S(1)} all-to-all(f32[256,1,1,512]{3,2,1,0:T(1,128)S(1)} %copy.18), channel_id=1, replica_groups=mesh['space'=12,'member'=64] {'member'}, dimensions={0} | all-to-all | bytes 1048576 | tf_op jit(solution)/shard_map/all_to_all | solution.py:86
  157.3 0.8 reshape.55
  (43 shorter events, 8.8 us)
Async XLA Ops:
  0.0 32.3 %copy-start = (f32[4,256,128]{2,1,0:T(8,128)S(1)}, f32[4,256,128]{2,1,0:T(8,128)}, u32[]{:S(2)}) copy-start(f32[4,256,128]{2,1,0:T(8,128)} %param.6) | copy-start | bytes 1572868
  0.0 32.3 %copy-start.1 = (f32[256,128]{1,0:T(8,128)S(1)}, f32[256,128]{1,0:T(8,128)}, u32[]{:S(2)}) copy-start(f32[256,128]{1,0:T(8,128)} %param.7) | copy-start | bytes 393220
  1.6 25.7 %collective-permute-start = (f32[4,256,1]{2,1,0:T(8,128)S(1)}, f32[4,256,1]{2,1,0:T(8,128)S(1)}, u32[]{:S(2)}, u32[]{:S(2)}) collective-permute-start(f32[4,256,1]{2,1,0:T(8,128)S(1)} %get-tuple-element.13), channel_id=1, source_target_pairs={{64,0},{128,64},{192,128},{256,192},{320,256},{384,320},{448,384},... | collective-permute-start | bytes 12296 | tf_op jit(solution)/shard_map/ppermute | solution.py:19
  16.7 15.6 %collective-permute-start.1 = (f32[4,256,1]{2,1,0:T(8,128)S(1)}, f32[4,256,1]{2,1,0:T(8,128)S(1)}, u32[]{:S(2)}, u32[]{:S(2)}) collective-permute-start(f32[4,256,1]{2,1,0:T(8,128)S(1)} %get-tuple-element.14), channel_id=1, source_target_pairs={{0,64},{64,128},{128,192},{192,256},{256,320},{320,384},{384,448},... | collective-permute-start | bytes 12296 | tf_op jit(solution)/shard_map/ppermute | solution.py:16
  33.1 13.6 %collective-permute-start.2 = (f32[4,256,1]{2,1,0:T(8,128)S(1)}, f32[4,256,1]{2,1,0:T(8,128)S(1)}, u32[]{:S(2)}, u32[]{:S(2)}) collective-permute-start(f32[4,256,1]{2,1,0:T(8,128)S(1)} %get-tuple-element.11), channel_id=1, source_target_pairs={{64,0},{128,64},{192,128},{256,192},{320,256},{384,320},{448,384},... | collective-permute-start | bytes 12296 | tf_op jit(solution)/shard_map/ppermute | solution.py:19
  35.0 14.8 %collective-permute-start.3 = (f32[4,256,1]{2,1,0:T(8,128)S(1)}, f32[4,256,1]{2,1,0:T(8,128)S(1)}, u32[]{:S(2)}, u32[]{:S(2)}) collective-permute-start(f32[4,256,1]{2,1,0:T(8,128)S(1)} %get-tuple-element.12), channel_id=1, source_target_pairs={{0,64},{64,128},{128,192},{192,256},{256,320},{320,384},{384,448},... | collective-permute-start | bytes 12296 | tf_op jit(solution)/shard_map/ppermute | solution.py:16
  50.6 12.7 %collective-permute-start.4 = (f32[4,256,1]{2,1,0:T(8,128)S(1)}, f32[4,256,1]{2,1,0:T(8,128)S(1)}, u32[]{:S(2)}, u32[]{:S(2)}) collective-permute-start(f32[4,256,1]{2,1,0:T(8,128)S(1)} %get-tuple-element.9), channel_id=1, source_target_pairs={{64,0},{128,64},{192,128},{256,192},{320,256},{384,320},{448,384},... | collective-permute-start | bytes 12296 | tf_op jit(solution)/shard_map/ppermute | solution.py:19
  52.5 13.9 %collective-permute-start.5 = (f32[4,256,1]{2,1,0:T(8,128)S(1)}, f32[4,256,1]{2,1,0:T(8,128)S(1)}, u32[]{:S(2)}, u32[]{:S(2)}) collective-permute-start(f32[4,256,1]{2,1,0:T(8,128)S(1)} %get-tuple-element.10), channel_id=1, source_target_pairs={{0,64},{64,128},{128,192},{192,256},{256,320},{320,384},{384,448},... | collective-permute-start | bytes 12296 | tf_op jit(solution)/shard_map/ppermute | solution.py:16
  67.2 11.9 %collective-permute-start.6 = (f32[4,256,1]{2,1,0:T(8,128)S(1)}, f32[4,256,1]{2,1,0:T(8,128)S(1)}, u32[]{:S(2)}, u32[]{:S(2)}) collective-permute-start(f32[4,256,1]{2,1,0:T(8,128)S(1)} %get-tuple-element.7), channel_id=1, source_target_pairs={{64,0},{128,64},{192,128},{256,192},{320,256},{384,320},{448,384},... | collective-permute-start | bytes 12296 | tf_op jit(solution)/shard_map/ppermute | solution.py:19
  69.2 13.1 %collective-permute-start.7 = (f32[4,256,1]{2,1,0:T(8,128)S(1)}, f32[4,256,1]{2,1,0:T(8,128)S(1)}, u32[]{:S(2)}, u32[]{:S(2)}) collective-permute-start(f32[4,256,1]{2,1,0:T(8,128)S(1)} %get-tuple-element.8), channel_id=1, source_target_pairs={{0,64},{64,128},{128,192},{192,256},{256,320},{320,384},{384,448},... | collective-permute-start | bytes 12296 | tf_op jit(solution)/shard_map/ppermute | solution.py:16
  84.0 15.3 %copy-start.2 = (s32[1,512]{1,0:T(1,128)S(1)}, s32[1,512]{1,0:T(1,128)}, u32[]{:S(2)}) copy-start(s32[1,512]{1,0:T(1,128)} %param.10) | copy-start | bytes 6148
  84.0 15.3 %copy-start.3 = (f32[1,512]{1,0:T(1,128)S(1)}, f32[1,512]{1,0:T(1,128)}, u32[]{:S(2)}) copy-start(f32[1,512]{1,0:T(1,128)} %param.9) | copy-start | bytes 6148
  84.0 31.9 %all-to-all-start = ((f32[4,64,1,512]{3,0,2,1:T(4,128)}), f32[4,64,1,512]{3,0,2,1:T(4,128)S(1)}, u32[]{:S(2)}, u32[]{:S(2)}) async-start(f32[4,64,1,512]{3,0,2,1:T(4,128)} %copy.16), calls=%async_computation | async-start | bytes 1048576 | tf_op jit(solution)/shard_map/all_to_all | solution.py:81
  121.6 0.7 copy-start.4
where the time goes:
time: 159 us; the launch traced here: 158 us
  waiting for transfers between devices  61.9 us (39%)
  starting transfers between devices  47.5 us (30%)
  blocking collectives  23.4 us (15%)
  local copies, waits for them, and re-layouts  11 us (7%)
  matrix products  9.98 us (6%)
  other arithmetic  2.52 us (2%)
  between operations  1.75 us (1%)
    ppermute x4, waiting for transfers between devices, padded_2(): lax.ppermute(lax.slice_in_dim(block, 0, width, axis=dim), axis, backward)  30.9 us
    all_to_all x1, blocking collectives, local(): lax.all_to_all(analysed_state, 'member', split_axis=0, concat_axis=1, til...  23.4 us
    ppermute x4, starting transfers between devices, padded_2(): lax.ppermute(lax.slice_in_dim(block, 0, width, axis=dim), axis, backward)  20.9 us
    all_to_all x1, waiting for transfers between devices, local(): lax.all_to_all(blocks, 'member', split_axis=1, concat_axis=0, tiled=True)  16.6 us
    all_to_all x1, starting transfers between devices, local(): lax.all_to_all(blocks, 'member', split_axis=1, concat_axis=0, tiled=True)  14.6 us
    ppermute x4, waiting for transfers between devices, padded_2(): lax.ppermute(lax.slice_in_dim(block, block.shape[dim] - width, None, axis...  14.5 us
    ppermute x4, starting transfers between devices, padded_2(): lax.ppermute(lax.slice_in_dim(block, block.shape[dim] - width, None, axis...  12 us
    gather x1, local copies, waits for them, and re-layouts, analyze(): ymean = jnp.take(mean, cells)  3.49 us
  transfers between devices with their start and end apart: 9, of which 9 were waited for; matrix products, arithmetic and copies ran while one was open for 0% of the time, Pallas kernels for 0%

commit v1 on v0

v1 whole, which is shorter than its diff:
```python
import functools
import jax
import jax.numpy as jnp
from jax import lax
from jax.experimental import pallas as pl
from jax.experimental.pallas import tpu as pltpu
from jax.sharding import PartitionSpec as P

SUBSTEPS = 4
NS_ITERS = 6
HEIGHT = 4
LANES = 128
MESH = pl.DeviceIdType.MESH
F32 = jnp.float32
BF16 = jnp.bfloat16


def halo_kernel(prior_ref, wind_ref, own_ref, left_ref, right_ref, send_sem, recv_sem):
    z = lax.axis_index("space")
    m = lax.axis_index("member")
    n = lax.axis_size("space")
    lft = lax.rem(z + n - 1, n)
    rgt = lax.rem(z + 1, n)
    barrier = pltpu.get_barrier_semaphore()
    for nb in (lft, rgt):
        pl.semaphore_signal(barrier, inc=1, device_id=(nb, m), device_id_type=MESH)
    rows = prior_ref.shape[0]
    own_ref[:, :rows] = pltpu.roll(prior_ref[...], SUBSTEPS, 1).T[:8, :]
    own_ref[:, rows:] = pltpu.roll(wind_ref[...], SUBSTEPS, 1).T[:8, :]
    pl.semaphore_wait(barrier, 2)
    to_right = pltpu.make_async_remote_copy(
        src_ref=own_ref, dst_ref=left_ref, send_sem=send_sem.at[0], recv_sem=recv_sem.at[0],
        device_id=(rgt, m), device_id_type=MESH)
    to_left = pltpu.make_async_remote_copy(
        src_ref=own_ref, dst_ref=right_ref, send_sem=send_sem.at[1], recv_sem=recv_sem.at[1],
        device_id=(lft, m), device_id_type=MESH)
    to_right.start()
    to_left.start()
    to_right.wait()
    to_left.wait()


def advance(center, east, west, ns, wind3):
    t = wind3 + 0.075 * jnp.tanh(center)
    return 0.4 * center + 0.1 * ns + 0.2 * (east + west) - t * (east - west)


def split(x):
    hi = x.astype(BF16)
    return hi, (x - hi.astype(F32)).astype(BF16)


def mul3(a, b):
    lhs = jnp.concatenate([a[0], a[0], a[1]], axis=1)
    rhs = jnp.concatenate([b[0], b[1], b[0]], axis=0)
    return jnp.dot(lhs, rhs, preferred_element_type=F32)


def main_kernel(count_ref, prior_ref, wind_ref, own_ref, left_ref, right_ref, value_ref, weight_ref,
                cells_ref, out_ref, edge, sbuf, rbuf, tbuf, obuf, pert_hi, pert_lo,
                send_sem, recv_sem):
    z = lax.axis_index("space")
    me = lax.axis_index("member")
    G = lax.axis_size("member")
    rows = prior_ref.shape[0]
    members = rows // (G * HEIGHT)
    ny = G * HEIGHT
    block = members * HEIGHT
    order = G * members
    barrier = pltpu.get_barrier_semaphore()

    def peer(o):
        return lax.rem(me + o, G)

    def greet(o, c):
        pl.semaphore_signal(barrier, inc=1, device_id=(z, peer(o)), device_id_type=MESH)
        return c

    lax.fori_loop(1, G, greet, 0)

    sub = lax.broadcasted_iota(jnp.int32, (8, rows), 0)
    row = lax.rem(lax.broadcasted_iota(jnp.int32, (8, rows), 1), ny)
    own = own_ref[...]
    low = lax.broadcasted_iota(jnp.int32, own.shape, 0) < 4
    left_all = jnp.where(low, left_ref[...], own)
    right_all = jnp.where(low, own, right_ref[...])
    strips = []
    for whole in (left_all, right_all):
        w3 = 0.3 * whole[:, rows:]
        strips.append((whole[:, :rows], jnp.concatenate([w3] * members, axis=1)))
    packed = jnp.zeros((8, rows), F32)
    for s in range(SUBSTEPS):
        (lu, lw), (ru, rw) = strips
        packed = jnp.where(sub == 2 * s + 1, pltpu.roll(lu, (2 * s + 1 - 3) % 8, 0), packed)
        packed = jnp.where(sub == 2 * s, pltpu.roll(ru, (2 * s - 4) % 8, 0), packed)
        if s < SUBSTEPS - 1:
            new = []
            for u, w in strips:
                north = jnp.where(row == ny - 1, 0.0, pltpu.roll(u, rows - 1, 1))
                south = jnp.where(row == 0, 0.0, pltpu.roll(u, 1, 1))
                new.append((advance(u, pltpu.roll(u, 7, 0), pltpu.roll(u, 1, 0), north + south, w), w))
            strips = new
    edge[:, :8] = packed.T

    lane = lax.broadcasted_iota(jnp.int32, (G, LANES), 1)
    patch = lax.broadcasted_iota(jnp.int32, (G, LANES), 0)
    wind3 = [0.3 * wind_ref[pl.ds(j, G, stride=HEIGHT), :] for j in range(HEIGHT)]

    def forecast(ml, carry):
        base = ml * ny
        c = [prior_ref[pl.ds(base + j, G, stride=HEIGHT), :] for j in range(HEIGHT)]
        h = [edge[pl.ds(base + j, G, stride=HEIGHT), :] for j in range(HEIGHT)]
        for s in range(SUBSTEPS):
            new = []
            for j in range(HEIGHT):
                hs = pltpu.roll(h[j], LANES - (2 * s + 1), 1)
                west = jnp.where(lane == 0, hs, pltpu.roll(c[j], 1, 1))
                east = jnp.where(lane == LANES - 1, hs, pltpu.roll(c[j], LANES - 1, 1))
                north = c[j + 1] if j < HEIGHT - 1 else jnp.where(
                    patch == G - 1, 0.0, pltpu.roll(c[0], G - 1, 0))
                south = c[j - 1] if j else jnp.where(patch == 0, 0.0, pltpu.roll(c[HEIGHT - 1], 1, 0))
                new.append(advance(c[j], east, west, north + south, wind3[j]))
            c = new
        for j in range(HEIGHT):
            sbuf[pl.ds(ml * HEIGHT + j, G, stride=block), :] = c[j]
        return carry

    lax.fori_loop(0, members, forecast, 0)
    pl.semaphore_wait(barrier, G - 1)

    def exchange(src, dst, k):
        def copy(o):
            to = peer(o)
            return pltpu.make_async_remote_copy(
                src_ref=src.at[pl.ds(pl.multiple_of(to * block, block), block), :],
                dst_ref=dst.at[pl.ds(pl.multiple_of(me * block, block), block), :],
                send_sem=send_sem.at[k], recv_sem=recv_sem.at[k],
                device_id=(z, to), device_id_type=MESH)

        def start(o, c):
            copy(o).start()
            return c

        lax.fori_loop(1, G, start, 0)
        mine = pl.ds(pl.multiple_of(me * block, block), block)
        dst[mine, :] = src[mine, :]

    def settle(src, k, sem):
        many = src.at[pl.ds(0, (G - 1) * block), :]
        pltpu.make_async_copy(many, many, sem.at[k]).wait()

    exchange(sbuf, rbuf, 0)

    slots = cells_ref.shape[1]
    live = lax.broadcasted_iota(jnp.int32, (1, slots), 1) < count_ref[0]
    wts = jnp.where(live, weight_ref[...], 0.0)
    wval = wts * value_ref[...]
    dsum = [jnp.zeros((8, LANES), F32) for _ in range(HEIGHT)]
    esum = [jnp.zeros((8, LANES), F32) for _ in range(HEIGHT)]
    cell_of = lax.broadcasted_iota(jnp.int32, (LANES, LANES), 1)
    for k in range(slots // LANES):
        part = slice(k * LANES, (k + 1) * LANES)
        cs = jnp.broadcast_to(cells_ref[:, part], (LANES, LANES)).T
        ws = jnp.broadcast_to(wts[:, part], (LANES, LANES)).T
        vs = jnp.broadcast_to(wval[:, part], (LANES, LANES)).T
        for j in range(HEIGHT):
            hit = cs == cell_of + j * LANES
            dsum[j] += jnp.sum(jnp.where(hit, ws, 0.0).reshape(LANES // 8, 8, LANES), axis=0)
            esum[j] += jnp.sum(jnp.where(hit, vs, 0.0).reshape(LANES // 8, 8, LANES), axis=0)
    dcell = [jnp.sum(x, axis=0, keepdims=True) for x in dsum]
    ecell = [jnp.sum(x, axis=0, keepdims=True) for x in esum]

    settle(rbuf, 0, recv_sem)

    mean = []
    rcell = []
    scaled = []
    for j in range(HEIGHT):
        x = jnp.concatenate(
            [rbuf[pl.ds(ml * HEIGHT + j, G, stride=block), :] for ml in range(members)], axis=0)
        mu = jnp.sum(x, axis=0, keepdims=True) * (1.0 / order)
        p = x - mu
        hi, lo = split(p)
        cols = slice(j * LANES, (j + 1) * LANES)
        pert_hi[:, cols] = hi
        pert_lo[:, cols] = lo
        scaled.append(split(p * dcell[j]))
        mean.append(mu)
        rcell.append(ecell[j] - dcell[j] * mu)
    a_hi = jnp.concatenate([s[0] for s in scaled], axis=1)
    a_lo = jnp.concatenate([s[1] for s in scaled], axis=1)
    nt = (((1,), (1,)), ((), ()))
    eye = (lax.broadcasted_iota(jnp.int32, (order, order), 0)
           == lax.broadcasted_iota(jnp.int32, (order, order), 1))
    gram = lax.dot_general(
        jnp.concatenate([a_hi, a_hi, a_lo], axis=1),
        jnp.concatenate([pert_hi[...], pert_lo[...], pert_hi[...]], axis=1),
        nt, preferred_element_type=F32)
    gram = gram + jnp.where(eye, order - 1.0, 0.0)
    total = jnp.sum(jnp.sum(gram * gram, axis=0, keepdims=True), axis=1, keepdims=True) + 1e-06
    scale = jnp.sqrt(total)
    y = gram / scale
    diag = jnp.where(eye, 1.5, 0.0)
    mid = diag - 0.5 * y
    ms = split(mid)
    y = mul3(split(y), ms)
    zmat = mid
    for step in range(1, NS_ITERS):
        ys, zs = split(y), split(zmat)
        ms = split(diag - 0.5 * mul3(zs, ys))
        if step < NS_ITERS - 1:
            y = mul3(ys, ms)
        zmat = mul3(zs, ms)
    root = zmat / jnp.sqrt(scale)
    dev = mul3(split(root), (pert_hi[...], pert_lo[...]))
    u = jnp.zeros((order, 1), F32)
    for j in range(HEIGHT):
        u = u + jnp.sum(dev[:, j * LANES:(j + 1) * LANES] * rcell[j], axis=1, keepdims=True)
    for j in range(HEIGHT):
        dj = dev[:, j * LANES:(j + 1) * LANES]
        shift = mean[j] + jnp.sum(dj * u, axis=0, keepdims=True)
        res = shift + jnp.sqrt(jnp.full((1, 1), order - 1.0, F32)) * dj
        for ml in range(members):
            tbuf[pl.ds(ml * HEIGHT + j, G, stride=block), :] = res[ml * G:(ml + 1) * G, :]

    exchange(tbuf, obuf, 1)
    settle(rbuf, 0, send_sem)
    settle(obuf, 1, recv_sem)
    for ml in range(members):
        for j in range(HEIGHT):
            out_ref[pl.ds(ml * ny + j, G, stride=HEIGHT), :] = obuf[
                pl.ds(ml * HEIGHT + j, G, stride=block), :]
    settle(obuf, 1, send_sem)


def local(prior_ensemble, wind, obs_value, obs_weight, observed_cell_value, obs_count):
    members, ny, columns = prior_ensemble.shape
    rows = members * ny
    order = members * lax.axis_size("member")
    prior = prior_ensemble.reshape(rows, columns)
    vmem = pl.BlockSpec(memory_space=pltpu.VMEM)
    strip = jax.ShapeDtypeStruct((8, rows + ny), F32)
    own, left, right = pl.pallas_call(
        halo_kernel,
        out_shape=(strip, strip, strip),
        in_specs=[vmem] * 2,
        out_specs=(vmem,) * 3,
        scratch_shapes=[pltpu.SemaphoreType.DMA((2,)), pltpu.SemaphoreType.DMA((2,))],
        compiler_params=pltpu.CompilerParams(collective_id=0, has_side_effects=True),
        name="halo",
    )(prior, wind)
    big = pltpu.VMEM((rows, LANES), F32)
    half = pltpu.VMEM((order, HEIGHT * LANES), BF16)
    out = pl.pallas_call(
        main_kernel,
        out_shape=jax.ShapeDtypeStruct((rows, columns), F32),
        in_specs=[pl.BlockSpec(memory_space=pltpu.SMEM)] + [vmem] * 8,
        out_specs=vmem,
        scratch_shapes=[big] * 5 + [half] * 2
        + [pltpu.SemaphoreType.DMA((2,)), pltpu.SemaphoreType.DMA((2,))],
        compiler_params=pltpu.CompilerParams(
            collective_id=1, has_side_effects=True, vmem_limit_bytes=40 * 1024 * 1024),
        name="forecast_analysis",
    )(obs_count, prior, wind, own, left, right, obs_value, obs_weight, observed_cell_value)
    return out.reshape(members, ny, columns)


def solution(mesh):
    in_specs = (
        P("member", None, "space"),
        P(None, "space"),
        P(("space", "member"), None),
        P(("space", "member"), None),
        P(("space", "member"), None),
        P(("space", "member")),
    )
    out_specs = P("member", None, "space")
    return jax.shard_map(local, mesh=mesh, in_specs=in_specs, out_specs=out_specs, check_vma=False)
```

time: 159 us -> 66.8 us (0.42)
  waiting for transfers between devices: 61.9 us -> 0 us
  Pallas kernels: 0 us -> 61.8 us
  starting transfers between devices: 47.5 us -> 0 us
  blocking collectives: 23.4 us -> 0 us
  matrix products: 9.98 us -> 0 us
  local copies, waits for them, and re-layouts: 11 us -> 3.8 us
  other arithmetic: 2.52 us -> 0 us
    pallas_call x0 -> x2, Pallas kernels: none -> 61.8 us  [the longest x1 44.2 us: local(): pl.pallas_call(main_kernel, out_shape=jax.ShapeDtypeStruct((rows, columns...]
    ppermute x8 -> x0, waiting for transfers between devices: 45.4 us -> none  [the longest x4 30.9 us: padded_2(): lax.ppermute(lax.slice_in_dim(block, 0, width, axis=dim), axis, backward)]
    ppermute x8 -> x0, starting transfers between devices: 32.9 us -> none  [the longest x4 20.9 us: padded_2(): lax.ppermute(lax.slice_in_dim(block, 0, width, axis=dim), axis, backward)]
    all_to_all x1 -> x0, blocking collectives: 23.4 us -> none  [local(): lax.all_to_all(analysed_state, 'member', split_axis=0, concat_axis=1, til...]
    all_to_all x1 -> x0, waiting for transfers between devices: 16.6 us -> none  [local(): lax.all_to_all(blocks, 'member', split_axis=1, concat_axis=0, tiled=True)]
    all_to_all x1 -> x0, starting transfers between devices: 14.6 us -> none  [local(): lax.all_to_all(blocks, 'member', split_axis=1, concat_axis=0, tiled=True)]
    dot_general x22 -> x0, matrix products: 9.98 us -> none  [the longest x6 2.27 us: inverse_root(): jnp.dot(lower, upper, precision=lax.Precision.HIGHEST)]
    gather x2 -> x0, local copies, waits for them, and re-layouts: 5.06 us -> none  [the longest x1 3.49 us: analyze(): ymean = jnp.take(mean, cells)]
  transfers between devices with their start and end apart: 9 -> 0, of which waited for: 9 -> 0; matrix products, arithmetic and copies ran while one was open for 0% -> 0% of each run, Pallas kernels for 0% -> 0%
where the time goes in v1:
time: 66.8 us; the launch traced here: 66.4 us
  Pallas kernels  61.8 us (93%)
  local copies, waits for them, and re-layouts  3.8 us (6%)
  between operations  0.79 us (1%)
    pallas_call x1, Pallas kernels, local(): pl.pallas_call(main_kernel, out_shape=jax.ShapeDtypeStruct((rows, columns...  44.2 us
    pallas_call x1, Pallas kernels, local(): pl.pallas_call(halo_kernel, out_shape=(strip, strip, strip), in_specs=[vm...  17.6 us
    unnamed x17, local copies, waits for them, and re-layouts  3.8 us

profile of v1, /device:TPU:1, one launch (start us, length us, event | category | flops | bytes accessed | tf_op | source)
XLA Modules:
  0.0 66.4 jit_solution(954434515115631937)
XLA Ops:
  0.0 0.0 copy-start
  0.7 0.0 copy-start.1
  0.7 0.0 copy-start.7
  0.7 17.6 %halo.1 = (f32[8,1280]{1,0:T(8,128)}, f32[8,1280]{1,0:T(8,128)}, f32[8,1280]{1,0:T(8,128)}) custom-call(f32[1024,128]{1,0:T(8,128)} %bitcast.2, f32[256,128]{1,0:T(8,128)} %wind_ref.3), custom_call_target="tpu_custom_call" | custom-call | tf_op jit(solution)/shard_map/halo/pallas_call | solution.py:243
  18.3 0.0 copy-start.6
  18.3 0.0 copy-start.5
  18.3 0.0 copy-done
  18.4 0.0 copy-done.1
  18.4 0.0 copy-done.7
  18.4 0.6 copy-done.6
  19.0 0.0 copy-done.5
  19.0 0.0 copy-start.2
  19.0 0.8 %copy-done.2 = f32[8,1280]{1,0:T(8,128)S(1)} copy-done((f32[8,1280]{1,0:T(8,128)S(1)}, f32[8,1280]{1,0:T(8,128)}, u32[]{:S(2)}) %copy-start.2) | copy-done | bytes 40984
  19.8 0.0 copy-start.3
  19.8 0.8 %copy-done.3 = f32[8,1280]{1,0:T(8,128)S(1)} copy-done((f32[8,1280]{1,0:T(8,128)S(1)}, f32[8,1280]{1,0:T(8,128)}, u32[]{:S(2)}) %copy-start.3) | copy-done | bytes 40984
  20.6 0.0 copy-start.4
  20.6 0.8 %copy-done.4 = f32[8,1280]{1,0:T(8,128)S(1)} copy-done((f32[8,1280]{1,0:T(8,128)S(1)}, f32[8,1280]{1,0:T(8,128)}, u32[]{:S(2)}) %copy-start.4) | copy-done | bytes 40984
  21.4 44.2 %forecast_analysis.1 = f32[1024,128]{1,0:T(8,128)S(1)} custom-call(s32[1]{0:T(128)S(6)} %copy.8.count_ref, f32[1024,128]{1,0:T(8,128)S(1)} %bitcast.3, f32[256,128]{1,0:T(8,128)S(1)} %copy-done.1, f32[8,1280]{1,0:T(8,128)S(1)} %copy-done.2, f32[8,1280]{1,0:T(8,128)S(1)} %copy-done.3, f32[8,1280]{1,0:T(8,128)S(1)} %copy-done.4, f32[1,512]{1,0:T(1,128)S(1)} %copy-done.5, ...), custom_call_target="tpu_custom_call" | custom-call | tf_op jit(solution)/shard_map/forecast_analysis/pallas_call | solution.py:254
  65.6 0.8 %copy.9 = f32[4,256,128]{2,1,0:T(8,128)} copy(f32[4,256,128]{2,1,0:T(8,128)S(1)} %bitcast.4) | data formatting | bytes 1048576
Async XLA Ops:
  0.0 18.3 %copy-start = (f32[4,256,128]{2,1,0:T(8,128)S(1)}, f32[4,256,128]{2,1,0:T(8,128)}, u32[]{:S(2)}) copy-start(f32[4,256,128]{2,1,0:T(8,128)} %param.6) | copy-start | bytes 1572868
  0.7 17.6 %copy-start.1 = (f32[256,128]{1,0:T(8,128)S(1)}, f32[256,128]{1,0:T(8,128)}, u32[]{:S(2)}) copy-start(f32[256,128]{1,0:T(8,128)} %wind_ref.3) | copy-start | bytes 393220
  0.7 17.6 %copy-start.7 = (s32[1,512]{1,0:T(1,128)S(1)}, s32[1,512]{1,0:T(1,128)}, u32[]{:S(2)}) copy-start(s32[1,512]{1,0:T(1,128)} %cells_ref.1) | copy-start | bytes 6148
  18.3 0.7 %copy-start.6 = (f32[1,512]{1,0:T(1,128)S(1)}, f32[1,512]{1,0:T(1,128)}, u32[]{:S(2)}) copy-start(f32[1,512]{1,0:T(1,128)} %weight_ref.1) | copy-start | bytes 6148
  18.3 0.7 %copy-start.5 = (f32[1,512]{1,0:T(1,128)S(1)}, f32[1,512]{1,0:T(1,128)}, u32[]{:S(2)}) copy-start(f32[1,512]{1,0:T(1,128)} %value_ref.1) | copy-start | bytes 6148
  19.0 0.8 %copy-start.2 = (f32[8,1280]{1,0:T(8,128)S(1)}, f32[8,1280]{1,0:T(8,128)}, u32[]{:S(2)}) copy-start(f32[8,1280]{1,0:T(8,128)} %get-tuple-element.8.own_ref) | copy-start | bytes 122884
  19.8 0.8 %copy-start.3 = (f32[8,1280]{1,0:T(8,128)S(1)}, f32[8,1280]{1,0:T(8,128)}, u32[]{:S(2)}) copy-start(f32[8,1280]{1,0:T(8,128)} %get-tuple-element.9.left_ref) | copy-start | bytes 122884
  20.6 0.8 %copy-start.4 = (f32[8,1280]{1,0:T(8,128)S(1)}, f32[8,1280]{1,0:T(8,128)}, u32[]{:S(2)}) copy-start(f32[8,1280]{1,0:T(8,128)} %get-tuple-element.10.right_ref) | copy-start | bytes 122884

commit v2 on v1

v2 whole, which is shorter than its diff:
```python
import functools
import jax
import jax.numpy as jnp
from jax import lax
from jax.experimental import pallas as pl
from jax.experimental.pallas import tpu as pltpu
from jax.sharding import PartitionSpec as P

SUBSTEPS = 4
NS_ITERS = 6
HEIGHT = 4
LANES = 128
VMEM_BYTES = 16 * 1024 * 1024
MESH = pl.DeviceIdType.MESH
F32 = jnp.float32
BF16 = jnp.bfloat16


def advance(center, east, west, ns, wind3):
    t = wind3 + 0.075 * jnp.tanh(center)
    return 0.4 * center + 0.1 * ns + 0.2 * (east + west) - t * (east - west)


def split(x):
    hi = x.astype(BF16)
    return hi, (x - hi.astype(F32)).astype(BF16)


def mul3(a, b):
    lhs = jnp.concatenate([a[0], a[0], a[1]], axis=1)
    rhs = jnp.concatenate([b[0], b[1], b[0]], axis=0)
    return jnp.dot(lhs, rhs, preferred_element_type=F32)


def main_kernel(count_hbm, prior_hbm, wind_hbm, value_hbm, weight_hbm, cells_hbm, obuf,
                count_ref, prior_ref, wind_ref, value_ref, weight_ref, cells_ref,
                own_ref, left_ref, right_ref, edge, sbuf, rbuf, tbuf, esend, erecv, pert_hi, pert_lo,
                in_sem, halo_send, halo_recv, send_sem, recv_sem, plane_sem, space_sem):
    z = lax.axis_index("space")
    me = lax.axis_index("member")
    Z = lax.axis_size("space")
    G = lax.axis_size("member")
    rows = prior_ref.shape[0]
    members = rows // (G * HEIGHT)
    ny = G * HEIGHT
    block = members * HEIGHT
    order = G * members
    lft = lax.rem(z + Z - 1, Z)
    rgt = lax.rem(z + 1, Z)
    core = lax.rem(me, 2)
    chip = me // 2
    loads = [pltpu.make_async_copy(src, dst, in_sem.at[i]) for i, (src, dst) in enumerate((
        (prior_hbm, prior_ref), (wind_hbm, wind_ref), (cells_hbm, cells_ref),
        (weight_hbm, weight_ref), (value_hbm, value_ref), (count_hbm, count_ref)))]
    for load in loads:
        load.start()
    barrier = pltpu.get_barrier_semaphore()

    def greet(o, c):
        to = lax.rem(chip + o, G // 2) * 2
        pl.semaphore_signal(barrier, inc=1, device_id=(z, to), device_id_type=MESH)
        return c

    lax.fori_loop(1, G // 2, greet, 0)

    @pl.when(core == 1)
    def _():
        pl.semaphore_signal(barrier, inc=1, device_id=(z, me - 1), device_id_type=MESH)

    for nb in (lft, rgt):
        pl.semaphore_signal(barrier, inc=1, device_id=(nb, chip * 2 + 1), device_id_type=MESH)

    patch = lax.broadcasted_iota(jnp.int32, (G, LANES), 0)
    loads[0].wait()
    loads[1].wait()
    wind3 = [0.3 * wind_ref[pl.ds(j, G, stride=HEIGHT), :] for j in range(HEIGHT)]

    def forecast(ml, carry):
        base = ml * ny
        c = [prior_ref[pl.ds(base + j, G, stride=HEIGHT), :] for j in range(HEIGHT)]
        for s in range(SUBSTEPS):
            new = []
            for j in range(HEIGHT):
                west = pltpu.roll(c[j], 1, 1)
                east = pltpu.roll(c[j], LANES - 1, 1)
                north = c[j + 1] if j < HEIGHT - 1 else jnp.where(
                    patch == G - 1, 0.0, pltpu.roll(c[0], G - 1, 0))
                south = c[j - 1] if j else jnp.where(patch == 0, 0.0, pltpu.roll(c[HEIGHT - 1], 1, 0))
                new.append(advance(c[j], east, west, north + south, wind3[j]))
            c = new
        for j in range(HEIGHT):
            sbuf[pl.ds(ml * HEIGHT + j, G, stride=block), :] = c[j]
        return carry

    lax.fori_loop(0, members, forecast, 0)

    @pl.when(core == 0)
    def _():
        pl.semaphore_wait(barrier, G - 1)
        pl.semaphore_signal(plane_sem, inc=1, device_id=(z, chip * 2 + 1), device_id_type=MESH)

    @pl.when(core == 1)
    def _():
        pl.semaphore_wait(plane_sem, 1)

    def exchange(make):
        ring = 8 if G >= 16 else G // 2
        columns = G // 2 // ring

        def both(k, c):
            t = lax.rem(k, ring)
            u = k // ring
            dy = ring // 2 + (1 - 2 * lax.rem(t, 2)) * ((t + 1) // 2)
            dx = columns // 2 + (1 - 2 * lax.rem(u, 2)) * ((u + 1) // 2)
            y = lax.rem(lax.rem(chip, ring) + dy, ring)
            x = lax.rem(chip // ring + dx, columns)
            to = (x * ring + y) * 2
            make(to + core).start()
            make(to + 1 - core).start()
            return c

        lax.fori_loop(0, G // 2 - 1, both, 0)
        make(chip * 2 + 1 - core).start()

    def blocks(src, dst, k):
        def make(to):
            return pltpu.make_async_remote_copy(
                src_ref=src.at[pl.ds(pl.multiple_of(to * block, block), block), :],
                dst_ref=dst.at[pl.ds(pl.multiple_of(me * block, block), block), :],
                send_sem=send_sem.at[k], recv_sem=recv_sem.at[k],
                device_id=(z, to), device_id_type=MESH)

        exchange(make)
        mine = pl.ds(pl.multiple_of(me * block, block), block)
        dst[mine, :] = src[mine, :]

    def settle(src, k, sem):
        many = src.at[pl.ds(0, (G - 1) * block), :]
        pltpu.make_async_copy(many, many, sem.at[k]).wait()

    blocks(sbuf, rbuf, 0)

    for ref, at in ((prior_ref, slice(0, rows)), (wind_ref, slice(rows, rows + ny))):
        turned = pltpu.roll(ref[...], SUBSTEPS, 1).T
        own_ref[0:8, at] = turned[0:8, :]
        own_ref[8:16, at] = turned[8:16, :]
        own_ref[16:24, at] = turned[LANES - 8:LANES, :]

    @pl.when(core == 1)
    def _():
        pl.semaphore_wait(barrier, 4)
        pl.semaphore_signal(space_sem, inc=1, device_id=(z, chip * 2), device_id_type=MESH)

    @pl.when(core == 0)
    def _():
        pl.semaphore_wait(space_sem, 1)

    halos = [pltpu.make_async_remote_copy(
        src_ref=own_ref.at[0:8, :], dst_ref=dst, send_sem=halo_send.at[k], recv_sem=halo_recv.at[k],
        device_id=(nb, me), device_id_type=MESH)
        for k, (dst, nb) in enumerate(((left_ref, rgt), (right_ref, lft)))]
    for halo in halos:
        halo.start()

    for load in loads[2:]:
        load.wait()
    slots = cells_ref.shape[1]
    live = lax.broadcasted_iota(jnp.int32, (1, slots), 1) < count_ref[0]
    wts = jnp.where(live, weight_ref[...], 0.0)
    wval = wts * value_ref[...]
    dsum = [jnp.zeros((8, LANES), F32) for _ in range(HEIGHT)]
    esum = [jnp.zeros((8, LANES), F32) for _ in range(HEIGHT)]
    cell_of = lax.broadcasted_iota(jnp.int32, (LANES, LANES), 1)
    for k in range(slots // LANES):
        part = slice(k * LANES, (k + 1) * LANES)
        cs = jnp.broadcast_to(cells_ref[:, part], (LANES, LANES)).T
        ws = jnp.broadcast_to(wts[:, part], (LANES, LANES)).T
        vs = jnp.broadcast_to(wval[:, part], (LANES, LANES)).T
        for j in range(HEIGHT):
            hit = cs == cell_of + j * LANES
            dsum[j] += jnp.sum(jnp.where(hit, ws, 0.0).reshape(LANES // 8, 8, LANES), axis=0)
            esum[j] += jnp.sum(jnp.where(hit, vs, 0.0).reshape(LANES // 8, 8, LANES), axis=0)
    dcell = [jnp.sum(x, axis=0, keepdims=True) for x in dsum]
    ecell = [jnp.sum(x, axis=0, keepdims=True) for x in esum]

    for halo in halos:
        halo.wait()
    low = lax.broadcasted_iota(jnp.int32, (8, rows + ny), 0) < 4
    first = own_ref[0:8, :]
    left_all = jnp.concatenate([jnp.where(low, left_ref[...], first), own_ref[8:16, :]], axis=0)
    right_all = jnp.concatenate([own_ref[16:24, :], jnp.where(low, first, right_ref[...])], axis=0)
    row = lax.rem(lax.broadcasted_iota(jnp.int32, (16, rows), 1), ny)
    ends = []
    for whole in (left_all, right_all):
        w3 = 0.3 * whole[:, rows:]
        w = jnp.concatenate([w3] * members, axis=1)
        x = whole[:, :rows]
        for s in range(SUBSTEPS):
            north = jnp.where(row == ny - 1, 0.0, pltpu.roll(x, rows - 1, 1))
            south = jnp.where(row == 0, 0.0, pltpu.roll(x, 1, 1))
            x = advance(x, pltpu.roll(x, 15, 0), pltpu.roll(x, 1, 0), north + south, w)
        ends.append(x)
    edge[:, :8] = jnp.where(low[:, :rows], ends[1][8:16, :], ends[0][0:8, :]).T
    lane = lax.broadcasted_iota(jnp.int32, (G, LANES), 1)
    packed = jnp.zeros((G, LANES), F32)
    for q in range(block):
        ml, j = q // HEIGHT, q % HEIGHT
        part = edge[pl.ds(ml * ny + j, G, stride=HEIGHT), :]
        packed = jnp.where(lane // 8 == q, pltpu.roll(part, 8 * q, 1), packed)
    esend[...] = packed.reshape(G, 1, LANES)

    def make_edge(to):
        return pltpu.make_async_remote_copy(
            src_ref=esend.at[pl.ds(to, 1)], dst_ref=erecv.at[pl.ds(me, 1)],
            send_sem=send_sem.at[2], recv_sem=recv_sem.at[2],
            device_id=(z, to), device_id_type=MESH)

    exchange(make_edge)
    erecv[pl.ds(me, 1)] = esend[pl.ds(me, 1)]
    settle(rbuf, 0, recv_sem)
    edges = erecv.at[pl.ds(0, G - 1)]
    pltpu.make_async_copy(edges, edges, recv_sem.at[2]).wait()
    got = erecv[...].reshape(G, LANES)
    outer = (lane < 4) | (lane >= LANES - 4)

    mean = []
    rcell = []
    scaled = []
    for j in range(HEIGHT):
        x = jnp.concatenate(
            [jnp.where(outer, pltpu.roll(got, (LANES - 4 - 8 * (ml * HEIGHT + j)) % LANES, 1),
                       rbuf[pl.ds(ml * HEIGHT + j, G, stride=block), :]) for ml in range(members)],
            axis=0)
        mu = jnp.sum(x, axis=0, keepdims=True) * (1.0 / order)
        p = x - mu
        hi, lo = split(p)
        cols = slice(j * LANES, (j + 1) * LANES)
        pert_hi[:, cols] = hi
        pert_lo[:, cols] = lo
        scaled.append(split(p * dcell[j]))
        mean.append(mu)
        rcell.append(ecell[j] - dcell[j] * mu)
    a_hi = jnp.concatenate([s[0] for s in scaled], axis=1)
    a_lo = jnp.concatenate([s[1] for s in scaled], axis=1)
    nt = (((1,), (1,)), ((), ()))
    eye = (lax.broadcasted_iota(jnp.int32, (order, order), 0)
           == lax.broadcasted_iota(jnp.int32, (order, order), 1))
    gram = lax.dot_general(
        jnp.concatenate([a_hi, a_hi, a_lo], axis=1),
        jnp.concatenate([pert_hi[...], pert_lo[...], pert_hi[...]], axis=1),
        nt, preferred_element_type=F32)
    gram = gram + jnp.where(eye, order - 1.0, 0.0)
    total = jnp.sum(jnp.sum(gram * gram, axis=0, keepdims=True), axis=1, keepdims=True) + 1e-06
    scale = jnp.sqrt(total)
    y = gram / scale
    diag = jnp.where(eye, 1.5, 0.0)
    mid = diag - 0.5 * y
    ms = split(mid)
    y = mul3(split(y), ms)
    zmat = mid
    for step in range(1, NS_ITERS):
        ys, zs = split(y), split(zmat)
        ms = split(diag - 0.5 * mul3(zs, ys))
        if step < NS_ITERS - 1:
            y = mul3(ys, ms)
        zmat = mul3(zs, ms)
    root = zmat / jnp.sqrt(scale)
    dev = mul3(split(root), (pert_hi[...], pert_lo[...]))
    u = jnp.zeros((order, 1), F32)
    for j in range(HEIGHT):
        u = u + jnp.sum(dev[:, j * LANES:(j + 1) * LANES] * rcell[j], axis=1, keepdims=True)
    for j in range(HEIGHT):
        dj = dev[:, j * LANES:(j + 1) * LANES]
        shift = mean[j] + jnp.sum(dj * u, axis=0, keepdims=True)
        res = shift + jnp.sqrt(jnp.full((1, 1), order - 1.0, F32)) * dj
        for ml in range(members):
            tbuf[pl.ds(ml * HEIGHT + j, G, stride=block), :] = res[ml * G:(ml + 1) * G, :]

    blocks(tbuf, obuf, 1)
    settle(sbuf, 0, send_sem)
    pltpu.make_async_copy(edges, edges, send_sem.at[2]).wait()
    settle(obuf, 1, recv_sem)
    settle(obuf, 1, send_sem)


def place_kernel(blocks_ref, out_hbm, tile, sem):
    rows = blocks_ref.shape[0]
    G = lax.axis_size("member")
    ny = G * HEIGHT
    members = rows // ny
    copies = []
    for ml in range(members):
        for j in range(HEIGHT):
            tile[pl.ds(ml * ny + j, G, stride=HEIGHT), :] = blocks_ref[
                pl.ds(ml * HEIGHT + j, G, stride=members * HEIGHT), :]
        span = pl.ds(ml * ny, ny)
        copies.append(pltpu.make_async_copy(tile.at[span, :], out_hbm.at[span, :], sem.at[ml]))
        copies[-1].start()
    for copy in copies:
        copy.wait()


def local(prior_ensemble, wind, obs_value, obs_weight, observed_cell_value, obs_count):
    members, ny, columns = prior_ensemble.shape
    rows = members * ny
    order = members * lax.axis_size("member")
    prior = prior_ensemble.reshape(rows, columns)
    vmem = pl.BlockSpec(memory_space=pltpu.VMEM)
    hbm = pl.BlockSpec(memory_space=pltpu.HBM)
    slots = obs_value.shape[1]
    big = pltpu.VMEM((rows, LANES), F32)
    strip = pltpu.VMEM((8, rows + ny), F32)
    half = pltpu.VMEM((order, HEIGHT * LANES), BF16)
    dma = pltpu.SemaphoreType.DMA
    blocks = pl.pallas_call(
        main_kernel,
        out_shape=pltpu.VMEM((rows, columns), F32),
        in_specs=[hbm] * 6,
        out_specs=vmem,
        scratch_shapes=[
            pltpu.SMEM((1,), jnp.int32), big, pltpu.VMEM((ny, LANES), F32),
            pltpu.VMEM((1, slots), F32), pltpu.VMEM((1, slots), F32),
            pltpu.VMEM((1, slots), jnp.int32)]
        + [pltpu.VMEM((24, rows + ny), F32)] + [strip] * 2 + [big] * 4
        + [pltpu.VMEM((order // members, 1, LANES), F32)] * 2 + [half] * 2
        + [dma((6,)), dma((2,)), dma((2,)), dma((3,)), dma((3,))]
        + [pltpu.SemaphoreType.REGULAR] * 2,
        compiler_params=pltpu.CompilerParams(
            collective_id=0, has_side_effects=True, vmem_limit_bytes=VMEM_BYTES),
        name="forecast_analysis",
    )(obs_count, *(pltpu.with_memory_space_constraint(a, pltpu.HBM) for a in (
        prior, wind, obs_value, obs_weight, observed_cell_value)))
    out = pl.pallas_call(
        place_kernel,
        out_shape=jax.ShapeDtypeStruct((rows, columns), F32),
        in_specs=[vmem],
        out_specs=hbm,
        scratch_shapes=[big, dma((members,))],
        compiler_params=pltpu.CompilerParams(vmem_limit_bytes=4 * 1024 * 1024),
        name="place",
    )(pltpu.with_memory_space_constraint(blocks, pltpu.VMEM))
    return out.reshape(members, ny, columns)


def solution(mesh):
    in_specs = (
        P("member", None, "space"),
        P(None, "space"),
        P(("space", "member"), None),
        P(("space", "member"), None),
        P(("space", "member"), None),
        P(("space", "member")),
    )
    out_specs = P("member", None, "space")
    return jax.shard_map(local, mesh=mesh, in_specs=in_specs, out_specs=out_specs, check_vma=False)
```

time: 66.8 us -> 54.1 us (0.81)
  Pallas kernels: 61.8 us -> 53.2 us
  local copies, waits for them, and re-layouts: 3.8 us -> 0 us
    pallas_call x2, Pallas kernels: 61.8 us -> 53.2 us  [the longest x1 52.4 us: local(): pl.pallas_call(main_kernel, out_shape=pltpu.VMEM((rows, columns), F32), i...]
    unnamed x17 -> x0, local copies, waits for them, and re-layouts: 3.8 us -> none
where the time goes in v2:
time: 54.1 us; the launch traced here: 53.9 us
  Pallas kernels  53.2 us (98%)
  between operations  0.66 us (1%)
    pallas_call x1, Pallas kernels, local(): pl.pallas_call(main_kernel, out_shape=pltpu.VMEM((rows, columns), F32), i...  52.4 us

profile of v2, /device:TPU:1, one launch (start us, length us, event | category | flops | bytes accessed | tf_op | source)
XLA Modules:
  0.0 53.9 jit_solution(10036940623998708450)
XLA Ops:
  0.7 52.4 %forecast_analysis.1.blocks_ref = f32[1024,128]{1,0:T(8,128)S(1)} custom-call(s32[1]{0:T(128)S(6)} %copy.7.count_hbm, f32[1024,128]{1,0:T(8,128)} %bitcast.2, f32[256,128]{1,0:T(8,128)} %wind_hbm.1, f32[1,512]{1,0:T(1,128)} %value_hbm.1, f32[1,512]{1,0:T(1,128)} %weight_hbm.1, s32[1,512]{1,0:T(1,128)} %cells_hbm.1), custom_call_target="tpu_custom_call" | custom-call | tf_op jit(solution)/shard_map/forecast_analysis/pallas_call | solution.py:315
  53.0 0.9 %place.1 = f32[1024,128]{1,0:T(8,128)} custom-call(f32[1024,128]{1,0:T(8,128)S(1)} %forecast_analysis.1.blocks_ref), custom_call_target="tpu_custom_call" | custom-call | tf_op jit(solution)/shard_map/place/pallas_call | solution.py:333

commit v3 on v2

--- a/solution.py
+++ b/solution.py
@@ -21,6 +21,10 @@
     return 0.4 * center + 0.1 * ns + 0.2 * (east + west) - t * (east - west)
 
 
+def turns(n):
+    return [n // 2 + (1 - 2 * (t % 2)) * ((t + 1) // 2) for t in range(n)]
+
+
 def split(x):
     hi = x.astype(BF16)
     return hi, (x - hi.astype(F32)).astype(BF16)
@@ -34,8 +38,8 @@
 
 def main_kernel(count_hbm, prior_hbm, wind_hbm, value_hbm, weight_hbm, cells_hbm, obuf,
                 count_ref, prior_ref, wind_ref, value_ref, weight_ref, cells_ref,
-                own_ref, left_ref, right_ref, edge, sbuf, rbuf, tbuf, esend, erecv, pert_hi, pert_lo,
-                in_sem, halo_send, halo_recv, send_sem, recv_sem, plane_sem, space_sem):
+                own_ref, left_ref, right_ref, edge, sbuf, lbuf, rbuf, tbuf, esend, erecv, pert_hi, pert_lo,
+                in_sem, halo_send, halo_recv, send_sem, recv_sem, plane_sem, space_sem, first_sem):
     z = lax.axis_index("space")
     me = lax.axis_index("member")
     Z = lax.axis_size("space")
@@ -55,17 +59,25 @@
     for load in loads:
         load.start()
     barrier = pltpu.get_barrier_semaphore()
-
-    def greet(o, c):
-        to = lax.rem(chip + o, G // 2) * 2
-        pl.semaphore_signal(barrier, inc=1, device_id=(z, to), device_id_type=MESH)
-        return c
-
-    lax.fori_loop(1, G // 2, greet, 0)
-
-    @pl.when(core == 1)
-    def _():
-        pl.semaphore_signal(barrier, inc=1, device_id=(z, me - 1), device_id_type=MESH)
+    first_in, herald, relay = 0, 2, 4
+
+    @pl.when(me != first_in)
+    def _():
+        def greet(c, carry):
+            @pl.when(c * 2 != me)
+            def _():
+                pl.semaphore_signal(barrier, inc=1, device_id=(z, c * 2), device_id_type=MESH)
+            return carry
+
+        lax.fori_loop(relay // 2, G // 2, greet, 0)
+
+    @pl.when(me == first_in)
+    def _():
+        pl.semaphore_signal(barrier, inc=1, device_id=(z, herald), device_id_type=MESH)
+
+    @pl.when(core == 0)
+    def _():
+        pl.semaphore_signal(barrier, inc=1, device_id=(z, me + 1), device_id_type=MESH)
 
     for nb in (lft, rgt):
         pl.semaphore_signal(barrier, inc=1, device_id=(nb, chip * 2 + 1), device_id_type=MESH)
@@ -92,45 +104,50 @@
             sbuf[pl.ds(ml * HEIGHT + j, G, stride=block), :] = c[j]
         return carry
 
-    lax.fori_loop(0, members, forecast, 0)
-
-    @pl.when(core == 0)
-    def _():
-        pl.semaphore_wait(barrier, G - 1)
-        pl.semaphore_signal(plane_sem, inc=1, device_id=(z, chip * 2 + 1), device_id_type=MESH)
-
-    @pl.when(core == 1)
-    def _():
-        pl.semaphore_wait(plane_sem, 1)
-
-    def exchange(make):
-        ring = 8 if G >= 16 else G // 2
-        columns = G // 2 // ring
-
-        def both(k, c):
-            t = lax.rem(k, ring)
-            u = k // ring
-            dy = ring // 2 + (1 - 2 * lax.rem(t, 2)) * ((t + 1) // 2)
+    ring = 8 if G >= 16 else G // 2
+    columns = G // 2 // ring
+    row_of = lax.rem(chip, ring)
+    column_of = chip // ring
+    near = [lax.rem(row_of + dy, ring) * 2 for dy in turns(ring)]
+    cores = (core, 1 - core)
+
+    across = turns(columns)
+    early = columns - 1
+
+    def exchange(make, first=0, last=columns, all_members=False):
+        def send(to):
+            if all_members:
+                make(to)
+            else:
+                pl.when(to != first_in)(lambda: make(to))
+
+        def column(u, c):
             dx = columns // 2 + (1 - 2 * lax.rem(u, 2)) * ((u + 1) // 2)
-            y = lax.rem(lax.rem(chip, ring) + dy, ring)
-            x = lax.rem(chip // ring + dx, columns)
-            to = (x * ring + y) * 2
-            make(to + core).start()
-            make(to + 1 - core).start()
+            there = lax.rem(column_of + dx, columns) * (ring * 2)
+            for y2 in near:
+                for c2 in cores:
+                    send(there + y2 + c2)
             return c
 
-        lax.fori_loop(0, G // 2 - 1, both, 0)
-        make(chip * 2 + 1 - core).start()
-
-    def blocks(src, dst, k):
+        lax.fori_loop(first, min(last, columns - 1), column, 0)
+        if last == columns:
+            here = column_of * (ring * 2)
+            for y2 in near[:-1]:
+                for c2 in cores:
+                    send(here + y2 + c2)
+            send(here + near[-1] + cores[1])
+
+    def block_copy(src, dst, k):
         def make(to):
-            return pltpu.make_async_remote_copy(
+            pltpu.make_async_remote_copy(
                 src_ref=src.at[pl.ds(pl.multiple_of(to * block, block), block), :],
                 dst_ref=dst.at[pl.ds(pl.multiple_of(me * block, block), block), :],
                 send_sem=send_sem.at[k], recv_sem=recv_sem.at[k],
-                device_id=(z, to), device_id_type=MESH)
-
-        exchange(make)
+                device_id=(z, to), device_id_type=MESH).start()
+
+        return make
+
+    def keep(src, dst):
         mine = pl.ds(pl.multiple_of(me * block, block), block)
         dst[mine, :] = src[mine, :]
 
@@ -138,7 +155,9 @@
         many = src.at[pl.ds(0, (G - 1) * block), :]
         pltpu.make_async_copy(many, many, sem.at[k]).wait()
 
-    blocks(sbuf, rbuf, 0)
+
+    def tell(sem, to):
+        pl.semaphore_signal(sem, inc=1, device_id=(z, to), device_id_type=MESH)
 
     for ref, at in ((prior_ref, slice(0, rows)), (wind_ref, slice(rows, rows + ny))):
         turned = pltpu.roll(ref[...], SUBSTEPS, 1).T
@@ -146,21 +165,112 @@
         own_ref[8:16, at] = turned[8:16, :]
         own_ref[16:24, at] = turned[LANES - 8:LANES, :]
 
-    @pl.when(core == 1)
-    def _():
-        pl.semaphore_wait(barrier, 4)
-        pl.semaphore_signal(space_sem, inc=1, device_id=(z, chip * 2), device_id_type=MESH)
-
-    @pl.when(core == 0)
-    def _():
-        pl.semaphore_wait(space_sem, 1)
-
     halos = [pltpu.make_async_remote_copy(
         src_ref=own_ref.at[0:8, :], dst_ref=dst, send_sem=halo_send.at[k], recv_sem=halo_recv.at[k],
         device_id=(nb, me), device_id_type=MESH)
         for k, (dst, nb) in enumerate(((left_ref, rgt), (right_ref, lft)))]
+
+    def send_halos():
+        @pl.when(core == 1)
+        def _():
+            pl.semaphore_wait(barrier, 5)
+            tell(space_sem, me - 1)
+
+        @pl.when(core == 0)
+        def _():
+            pl.semaphore_wait(space_sem, 1)
+
+        for halo in halos:
+            halo.start()
+
+    @pl.when(z != 0)
+    def _():
+        send_halos()
+
+    lax.fori_loop(0, members, forecast, 0)
+
+    @pl.when((core == 0) & (me >= relay))
+    def _():
+        pl.semaphore_wait(barrier, G - 2)
+        tell(plane_sem, me + 1)
+
+        @pl.when(me == relay)
+        def _():
+            for to in range(1, relay):
+                tell(plane_sem, to)
+
+    @pl.when((core == 1) | (me == herald))
+    def _():
+        pl.semaphore_wait(plane_sem, 1)
+
+    @pl.when(me == herald)
+    def _():
+        pl.semaphore_wait(barrier, 1)
+
+        def pass_on(o, carry):
+            tell(first_sem, lax.rem(me + o, G))
+            return carry
+
+        lax.fori_loop(1, G, pass_on, 0)
+
+    @pl.when(me == first_in)
+    def _():
+        pl.semaphore_wait(first_sem, 1)
+
+    exchange(block_copy(sbuf, rbuf, 0), 0, early)
+
+    @pl.when(z == 0)
+    def _():
+        send_halos()
+
+
     for halo in halos:
-        halo.start()
+        halo.wait()
+    low = lax.broadcasted_iota(jnp.int32, (8, rows + ny), 0) < 4
+    first = own_ref[0:8, :]
+    left_all = jnp.concatenate([jnp.where(low, left_ref[...], first), own_ref[8:16, :]], axis=0)
+    right_all = jnp.concatenate([own_ref[16:24, :], jnp.where(low, first, right_ref[...])], axis=0)
+    row = lax.rem(lax.broadcasted_iota(jnp.int32, (16, rows), 1), ny)
+    ends = []
+    for whole in (left_all, right_all):
+        w3 = 0.3 * whole[:, rows:]
+        w = jnp.concatenate([w3] * members, axis=1)
+        x = whole[:, :rows]
+        for s in range(SUBSTEPS):
+            north = jnp.where(row == ny - 1, 0.0, pltpu.roll(x, rows - 1, 1))
+            south = jnp.where(row == 0, 0.0, pltpu.roll(x, 1, 1))
+            x = advance(x, pltpu.roll(x, 15, 0), pltpu.roll(x, 1, 0), north + south, w)
+        ends.append(x)
+    edge[:, :8] = jnp.where(low[:, :rows], ends[1][8:16, :], ends[0][0:8, :]).T
+    lane = lax.broadcasted_iota(jnp.int32, (G, LANES), 1)
+    outer = (lane < 4) | (lane >= LANES - 4)
+    parts = [edge[pl.ds(q // HEIGHT * ny + q % HEIGHT, G, stride=HEIGHT), :] for q in range(block)]
+    packed = jnp.zeros((G, LANES), F32)
+    for q in range(block):
+        packed = jnp.where(lane // 8 == q, pltpu.roll(parts[q], 8 * q, 1), packed)
+    esend[...] = packed.reshape(G, 1, LANES)
+
+    def make_edge(to):
+        pltpu.make_async_remote_copy(
+            src_ref=esend.at[pl.ds(to, 1)], dst_ref=erecv.at[pl.ds(me, 1)],
+            send_sem=send_sem.at[2], recv_sem=recv_sem.at[2],
+            device_id=(z, to), device_id_type=MESH).start()
+
+    exchange(make_edge, 0, early)
+    for q in range(block):
+        mine = pl.ds(q, G, stride=block)
+        lbuf[mine, :] = jnp.where(outer, pltpu.roll(parts[q], LANES - 4, 1), sbuf[mine, :])
+
+    @pl.when((me != first_in) & (me != herald))
+    def _():
+        pl.semaphore_wait(first_sem, 1)
+
+    @pl.when(me != first_in)
+    def _():
+        block_copy(lbuf, rbuf, 0)(first_in)
+
+    exchange(block_copy(lbuf, rbuf, 0), early)
+    keep(lbuf, rbuf)
 
     for load in loads[2:]:
         load.wait()
@@ -183,45 +293,17 @@
     dcell = [jnp.sum(x, axis=0, keepdims=True) for x in dsum]
     ecell = [jnp.sum(x, axis=0, keepdims=True) for x in esum]
 
-    for halo in halos:
-        halo.wait()
-    low = lax.broadcasted_iota(jnp.int32, (8, rows + ny), 0) < 4
-    first = own_ref[0:8, :]
-    left_all = jnp.concatenate([jnp.where(low, left_ref[...], first), own_ref[8:16, :]], axis=0)
-    right_all = jnp.concatenate([own_ref[16:24, :], jnp.where(low, first, right_ref[...])], axis=0)
-    row = lax.rem(lax.broadcasted_iota(jnp.int32, (16, rows), 1), ny)
-    ends = []
-    for whole in (left_all, right_all):
-        w3 = 0.3 * whole[:, rows:]
-        w = jnp.concatenate([w3] * members, axis=1)
-        x = whole[:, :rows]
-        for s in range(SUBSTEPS):
-            north = jnp.where(row == ny - 1, 0.0, pltpu.roll(x, rows - 1, 1))
-            south = jnp.where(row == 0, 0.0, pltpu.roll(x, 1, 1))
-            x = advance(x, pltpu.roll(x, 15, 0), pltpu.roll(x, 1, 0), north + south, w)
-        ends.append(x)
-    edge[:, :8] = jnp.where(low[:, :rows], ends[1][8:16, :], ends[0][0:8, :]).T
-    lane = lax.broadcasted_iota(jnp.int32, (G, LANES), 1)
-    packed = jnp.zeros((G, LANES), F32)
-    for q in range(block):
-        ml, j = q // HEIGHT, q % HEIGHT
-        part = edge[pl.ds(ml * ny + j, G, stride=HEIGHT), :]
-        packed = jnp.where(lane // 8 == q, pltpu.roll(part, 8 * q, 1), packed)
-    esend[...] = packed.reshape(G, 1, LANES)
-
-    def make_edge(to):
-        return pltpu.make_async_remote_copy(
-            src_ref=esend.at[pl.ds(to, 1)], dst_ref=erecv.at[pl.ds(me, 1)],
-            send_sem=send_sem.at[2], recv_sem=recv_sem.at[2],
-            device_id=(z, to), device_id_type=MESH)
-
-    exchange(make_edge)
-    erecv[pl.ds(me, 1)] = esend[pl.ds(me, 1)]
     settle(rbuf, 0, recv_sem)
-    edges = erecv.at[pl.ds(0, G - 1)]
-    pltpu.make_async_copy(edges, edges, recv_sem.at[2]).wait()
+    edges = erecv.at[pl.ds(0, early * ring * 2)]
+    if early:
+        @pl.when(me != first_in)
+        def _():
+            pltpu.make_async_copy(edges, edges, recv_sem.at[2]).wait()
+
     got = erecv[...].reshape(G, LANES)
-    outer = (lane < 4) | (lane >= LANES - 4)
+    ahead = lax.rem(column_of - lax.broadcasted_iota(jnp.int32, (G, LANES), 0) // (ring * 2) + columns, columns)
+    ahead = jnp.where(me == first_in, columns, ahead)
+    outer &= functools.reduce(jnp.logical_or, [ahead == dx for dx in across[:early]], ahead < 0)
 
     mean = []
     rcell = []
@@ -276,9 +358,20 @@
         for ml in range(members):
             tbuf[pl.ds(ml * HEIGHT + j, G, stride=block), :] = res[ml * G:(ml + 1) * G, :]
 
-    blocks(tbuf, obuf, 1)
+    exchange(block_copy(tbuf, obuf, 1), all_members=True)
+    keep(tbuf, obuf)
     settle(sbuf, 0, send_sem)
-    pltpu.make_async_copy(edges, edges, send_sem.at[2]).wait()
+    if early:
+        some = erecv.at[pl.ds(0, early * ring * 2 - 1)]
+
+        @pl.when(column_of != 0)
+        def _():
+            pltpu.make_async_copy(some, some, send_sem.at[2]).wait()
+
+        @pl.when(column_of == 0)
+        def _():
+            pltpu.make_async_copy(edges, edges, send_sem.at[2]).wait()
+
     settle(obuf, 1, recv_sem)
     settle(obuf, 1, send_sem)
 
@@ -321,10 +414,10 @@
             pltpu.SMEM((1,), jnp.int32), big, pltpu.VMEM((ny, LANES), F32),
             pltpu.VMEM((1, slots), F32), pltpu.VMEM((1, slots), F32),
             pltpu.VMEM((1, slots), jnp.int32)]
-        + [pltpu.VMEM((24, rows + ny), F32)] + [strip] * 2 + [big] * 4
+        + [pltpu.VMEM((24, rows + ny), F32)] + [strip] * 2 + [big] * 5
         + [pltpu.VMEM((order // members, 1, LANES), F32)] * 2 + [half] * 2
         + [dma((6,)), dma((2,)), dma((2,)), dma((3,)), dma((3,))]
-        + [pltpu.SemaphoreType.REGULAR] * 2,
+        + [pltpu.SemaphoreType.REGULAR] * 3,
         compiler_params=pltpu.CompilerParams(
             collective_id=0, has_side_effects=True, vmem_limit_bytes=VMEM_BYTES),
         name="forecast_analysis",

time: 54.1 us -> 48.7 us (0.900)
  Pallas kernels: 53.2 us -> 47.9 us
    pallas_call x1, Pallas kernels: 52.4 us -> 47 us  [local(): pl.pallas_call(main_kernel, out_shape=pltpu.VMEM((rows, columns), F32), i...]
where the time goes in v3:
time: 48.7 us; the launch traced here: 48.5 us
  Pallas kernels  47.9 us (98%)
  between operations  0.66 us (1%)
    pallas_call x1, Pallas kernels, local(): pl.pallas_call(main_kernel, out_shape=pltpu.VMEM((rows, columns), F32), i...  47 us

profile of v3, /device:TPU:1, one launch (start us, length us, event | category | flops | bytes accessed | tf_op | source)
XLA Modules:
  0.0 48.5 jit_solution(12402152258819952377)
XLA Ops:
  0.7 47.0 %forecast_analysis.1.blocks_ref = f32[1024,128]{1,0:T(8,128)S(1)} custom-call(s32[1]{0:T(128)S(6)} %copy.7.count_hbm, f32[1024,128]{1,0:T(8,128)} %bitcast.2, f32[256,128]{1,0:T(8,128)} %wind_hbm.1, f32[1,512]{1,0:T(1,128)} %value_hbm.1, f32[1,512]{1,0:T(1,128)} %weight_hbm.1, s32[1,512]{1,0:T(1,128)} %cells_hbm.1), custom_call_target="tpu_custom_call" | custom-call | tf_op jit(solution)/shard_map/forecast_analysis/pallas_call | solution.py:408
  47.7 0.9 %place.1 = f32[1024,128]{1,0:T(8,128)} custom-call(f32[1024,128]{1,0:T(8,128)S(1)} %forecast_analysis.1.blocks_ref), custom_call_target="tpu_custom_call" | custom-call | tf_op jit(solution)/shard_map/place/pallas_call | solution.py:426
